TPU v7x, 32 devices: a whole 2x2x4 slice. The times are simulated.
32 devices in a mesh: fsdp: 8 (over z, core), seq: 4 (over y, x).
Axes of the slice: x: 2, y: 2, z: 4, core: 2. Of those that a mesh axis runs over, the one named last changes fastest.
Arguments:
- inputs: bfloat16 [8, 1024, 2048], P('fsdp', 'seq'), may hold values from -6 to 6
- cotangent: bfloat16 [8, 1024, 2048], P('fsdp', 'seq'), may hold values from -6 to 6
- norm1_gain: bfloat16 [2048], P('fsdp'), may hold values from 0.5 to 1.5
- w_qkv: bfloat16 [2048, 6144], P('fsdp'), may hold values from -0.125 to 0.125
- w_beta: bfloat16 [2048, 16], P('fsdp'), may hold values from -0.125 to 0.125
- conv_weight: bfloat16 [2048, 12], P('fsdp'), may hold values from -3 to 3
- out_gain: bfloat16 [128], replicated, may hold values from 0.5 to 1.5
- w_out: bfloat16 [2048, 2048], P('fsdp'), may hold values from -0.125 to 0.125
- norm2_gain: bfloat16 [2048], P('fsdp'), may hold values from 0.5 to 1.5
- w_gate_up: bfloat16 [2048, 11264], P('fsdp'), may hold values from -0.125 to 0.125
- w_down: bfloat16 [5632, 2048], P('fsdp'), may hold values from -0.15625 to 0.15625
Outputs:
- output: bfloat16 [8, 1024, 2048], P('fsdp', 'seq')
- grad_input: float32 [8, 1024, 2048], P('fsdp', 'seq')
- grad_norm1_gain: float32 [2048], P('fsdp')
- grad_w_qkv: float32 [2048, 6144], P('fsdp')
- grad_w_beta: float32 [2048, 16], P('fsdp')
- grad_conv_weight: float32 [2048, 12], P('fsdp')
- grad_out_gain: float32 [128], replicated
- grad_w_out: float32 [2048, 2048], P('fsdp')
- grad_norm2_gain: float32 [2048], P('fsdp')
- grad_w_gate_up: float32 [2048, 11264], P('fsdp')
- grad_w_down: float32 [5632, 2048], P('fsdp')
All inputs are finite; a program needn't handle non-finite values.
Results may differ from a plain program's by a relative error of at most 0.023.
Values may be sent and summed in bfloat16 or wider, within the bound.
A program may use at most 448 MiB of HBM per device.

v0:
```python
import jax
import jax.numpy as jnp
from jax import lax
from jax.sharding import PartitionSpec as P

H = 16
DK = 128
SPAN = 64
EPS = 1e-06
HIGH = lax.Precision.HIGHEST


def from_behind(array, axis, by):
    devices = lax.axis_size(axis)
    pairs = [(i, i + by) for i in range(devices) if 0 <= i + by < devices]
    return lax.ppermute(array, axis, pairs)


def rms_scale(values, gain):
    return values * lax.rsqrt(jnp.mean(values * values, axis=-1, keepdims=True) + EPS) * gain


def conv_table(conv_full):
    width = conv_full.shape[0]
    tap_count = conv_full.shape[1] // 3
    return (
        conv_full.astype(jnp.float32)
        .reshape(width, 3, tap_count)
        .transpose(1, 0, 2)
        .reshape(3 * width, tap_count)
    )


def pre_mix(extended, table, beta_logits):
    tap_count = table.shape[1]
    length = extended.shape[1] - tap_count + 1
    sequences = extended.shape[0]
    width = extended.shape[2] // 3
    mixed = extended[:, 0:length, :] * table[:, 0]
    for tap_index in range(1, tap_count):
        mixed = mixed + extended[:, tap_index : tap_index + length, :] * table[:, tap_index]
    active = jax.nn.silu(mixed)
    query = active[:, :, :width].reshape(sequences, length, H, DK) * DK ** (-0.5)
    key = active[:, :, width : 2 * width].reshape(sequences, length, H, DK)
    key = key * lax.rsqrt(jnp.sum(key * key, axis=-1, keepdims=True) + EPS)
    value = active[:, :, 2 * width :].reshape(sequences, length, H, DK)
    return (query, key, value, jax.nn.sigmoid(beta_logits))


def delta_rule(query, key, value, beta):
    sequences, length, heads, depth = query.shape
    count = length // SPAN

    def blocks(array):
        return array.reshape(sequences, count, SPAN, heads, -1).transpose(1, 0, 3, 2, 4)

    q_blocks = blocks(query)
    k_blocks = blocks(key)
    v_blocks = blocks(value)
    b_blocks = blocks(beta[..., None])
    gram = jnp.einsum("nshcd,nshmd->nshcm", k_blocks, k_blocks, precision=HIGH)
    below = jnp.tril(jnp.ones((SPAN, SPAN), jnp.float32), -1)
    inclusive = jnp.tril(jnp.ones((SPAN, SPAN), jnp.float32))
    system = jnp.eye(SPAN, dtype=jnp.float32) + below * (b_blocks * gram)
    targets = jnp.concatenate([b_blocks * k_blocks, b_blocks * v_blocks], axis=-1)
    solved = lax.linalg.triangular_solve(
        system, targets, left_side=True, lower=True, unit_diagonal=True
    )
    wy_key = solved[..., :depth]
    wy_value = solved[..., depth:]
    within = inclusive * jnp.einsum("nshcd,nshmd->nshcm", q_blocks, k_blocks, precision=HIGH)

    def advance(state, pieces):
        key_part, value_part, query_part, key_raw, attend = pieces
        fresh = value_part - jnp.einsum("shcd,shde->shce", key_part, state, precision=HIGH)
        result = jnp.einsum("shcd,shde->shce", query_part, state, precision=HIGH)
        result = result + jnp.einsum("shcm,shme->shce", attend, fresh, precision=HIGH)
        state = state + jnp.einsum("shcd,shce->shde", key_raw, fresh, precision=HIGH)
        return (state, result)

    start = jnp.zeros((sequences, heads, depth, value.shape[-1]), jnp.float32)
    final, outputs = lax.scan(advance, start, (wy_key, wy_value, q_blocks, k_blocks, within))
    return outputs.transpose(1, 0, 3, 2, 4).reshape(sequences, length, heads, -1)


def row_term(left, right):

    def term(start, count):
        return lax.dot_general(
            left, right, (((0,), (0,)), ((), ())), preferred_element_type=jnp.float32
        )

    return term


def reduce_rows(term, total_rows):
    shards = lax.axis_size("fsdp")
    summed = lax.psum_scatter(
        term(jnp.int32(0), total_rows // shards * lax.axis_size("fsdp")).astype(jnp.bfloat16),
        "fsdp",
        scatter_dimension=0,
        tiled=True,
    )
    return lax.psum(summed, "seq").astype(jnp.float32)


def against(left, right):
    return lax.dot_general(
        left, right, (((1,), (1,)), ((), ())), preferred_element_type=jnp.float32
    )


def per_device(
    inputs,
    cotangent,
    norm1_gain,
    w_qkv,
    w_beta,
    conv_weight,
    out_gain,
    w_out,
    norm2_gain,
    w_gate_up,
    w_down,
):
    gathered = (
        lax.all_gather(norm1_gain, "fsdp", axis=0, tiled=True),
        lax.all_gather(w_qkv, "fsdp", axis=0, tiled=True),
        lax.all_gather(w_beta, "fsdp", axis=0, tiled=True),
        lax.all_gather(conv_weight, "fsdp", axis=0, tiled=True),
        lax.all_gather(w_out, "fsdp", axis=0, tiled=True),
        lax.all_gather(norm2_gain, "fsdp", axis=0, tiled=True),
        lax.all_gather(w_gate_up, "fsdp", axis=0, tiled=True),
    )
    gain_first, qkv_full, beta_full, conv_full, out_full, gain_second, gate_up_full = gathered
    down_full = lax.all_gather(w_down, "fsdp", axis=0, tiled=True)
    sequences, block, width = inputs.shape
    tokens = sequences * block
    hidden_width = down_full.shape[0]
    edge_rows = conv_full.shape[1] // 3 - 1
    residual = inputs.astype(jnp.float32).reshape(tokens, width)
    first_normed, first_back = jax.vjp(rms_scale, residual, gain_first.astype(jnp.float32))
    normed_first = first_normed.astype(jnp.bfloat16)
    projected = jnp.dot(normed_first, qkv_full, preferred_element_type=jnp.float32)
    projected = projected.astype(jnp.bfloat16).reshape(sequences, block, 3 * width)
    beta_logits = jnp.dot(normed_first, beta_full, preferred_element_type=jnp.float32).reshape(
        sequences, block, -1
    )
    before = from_behind(projected[:, block - edge_rows :, :], "seq", 1)
    extended = jnp.concatenate([before, projected], axis=1).astype(jnp.float32)
    table = conv_table(conv_full)
    mixer_inputs, mixer_back = jax.vjp(pre_mix, extended, table, beta_logits)
    sent_query = mixer_inputs[0].astype(jnp.bfloat16)
    sent_key = mixer_inputs[1].astype(jnp.bfloat16)
    sent_value = mixer_inputs[2].astype(jnp.bfloat16)
    sent_beta = mixer_inputs[3].astype(jnp.bfloat16)
    query, key, value, beta = (
        lax.all_to_all(sent_query, "seq", split_axis=2, concat_axis=1, tiled=True),
        lax.all_to_all(sent_key, "seq", split_axis=2, concat_axis=1, tiled=True),
        lax.all_to_all(sent_value, "seq", split_axis=2, concat_axis=1, tiled=True),
        lax.all_to_all(sent_beta, "seq", split_axis=2, concat_axis=1, tiled=True),
    )
    heads_out, delta_back = jax.vjp(
        delta_rule,
        query.astype(jnp.float32),
        key.astype(jnp.float32),
        value.astype(jnp.float32),
        beta.astype(jnp.float32),
    )
    returned = lax.all_to_all(
        heads_out.astype(jnp.bfloat16), "seq", split_axis=1, concat_axis=2, tiled=True
    )
    normed_heads, heads_back = jax.vjp(
        rms_scale, returned.astype(jnp.float32), out_gain.astype(jnp.float32)
    )
    attn_in = normed_heads.astype(jnp.bfloat16).reshape(tokens, width)
    middle = residual + jnp.dot(attn_in, out_full, preferred_element_type=jnp.float32)
    second_normed, second_back = jax.vjp(rms_scale, middle, gain_second.astype(jnp.float32))
    ffn_in = second_normed.astype(jnp.bfloat16)
    gate_up = jnp.dot(ffn_in, gate_up_full, preferred_element_type=jnp.float32)
    gate = gate_up[:, :hidden_width]
    upward = gate_up[:, hidden_width:]
    sigma = jax.nn.sigmoid(gate)
    hidden = (gate * sigma * upward).astype(jnp.bfloat16)
    result = middle + jnp.dot(hidden, down_full, preferred_element_type=jnp.float32)
    output = result.astype(jnp.bfloat16).reshape(sequences, block, width)
    upstream = cotangent.reshape(tokens, width)
    grad_down = reduce_rows(row_term(hidden, upstream), hidden_width)
    grad_hidden = against(upstream, down_full)
    grad_gate = grad_hidden * upward * sigma * (1.0 + gate * (1.0 - sigma))
    grad_up = grad_hidden * gate * sigma
    grad_gate_up = jnp.concatenate([grad_gate, grad_up], axis=1).astype(jnp.bfloat16)
    grad_w_gate_up = reduce_rows(row_term(ffn_in, grad_gate_up), width)
    grad_ffn_in = against(grad_gate_up, gate_up_full)
    grad_middle_norm, grad_gain_second = second_back(grad_ffn_in)
    grad_middle = upstream.astype(jnp.float32) + grad_middle_norm
    grad_branch = grad_middle.astype(jnp.bfloat16)
    grad_w_out = reduce_rows(row_term(attn_in, grad_branch), width)
    grad_attn_in = against(grad_branch, out_full).reshape(sequences, block, H, DK)
    grad_returned, grad_gain_heads = heads_back(grad_attn_in)
    grad_heads = lax.all_to_all(
        grad_returned.astype(jnp.bfloat16), "seq", split_axis=2, concat_axis=1, tiled=True
    )
    grad_query, grad_key, grad_value, grad_beta = delta_back(grad_heads.astype(jnp.float32))
    back_query, back_key, back_value, back_beta = (
        lax.all_to_all(
            grad_query.astype(jnp.bfloat16), "seq", split_axis=1, concat_axis=2, tiled=True
        ),
        lax.all_to_all(
            grad_key.astype(jnp.bfloat16), "seq", split_axis=1, concat_axis=2, tiled=True
        ),
        lax.all_to_all(
            grad_value.astype(jnp.bfloat16), "seq", split_axis=1, concat_axis=2, tiled=True
        ),
        lax.all_to_all(
            grad_beta.astype(jnp.bfloat16), "seq", split_axis=1, concat_axis=2, tiled=True
        ),
    )
    grad_extended, grad_table, grad_logits = mixer_back(
        (
            back_query.astype(jnp.float32),
            back_key.astype(jnp.float32),
            back_value.astype(jnp.float32),
            back_beta.astype(jnp.float32),
        )
    )
    after = from_behind(grad_extended[:, :edge_rows, :].astype(jnp.bfloat16), "seq", -1).astype(
        jnp.float32
    )
    grad_projected = grad_extended[:, edge_rows:, :]
    grad_projected = grad_projected.at[:, block - edge_rows :, :].add(after)
    grad_proj_low = grad_projected.astype(jnp.bfloat16).reshape(tokens, 3 * width)
    grad_logits_low = grad_logits.astype(jnp.bfloat16).reshape(tokens, -1)
    grad_w_qkv = reduce_rows(row_term(normed_first, grad_proj_low), width)
    grad_beta_full = lax.dot_general(
        normed_first, grad_logits_low, (((0,), (0,)), ((), ())), preferred_element_type=jnp.float32
    )
    grad_normed_first = against(grad_proj_low, qkv_full) + against(grad_logits_low, beta_full)
    grad_residual_norm, grad_gain_first = first_back(grad_normed_first)
    grad_input = (grad_middle + grad_residual_norm).reshape(sequences, block, width)
    grad_conv = grad_table.reshape(3, width, -1).transpose(1, 0, 2).reshape(width, -1)
    summed = lax.psum(
        (grad_gain_first, grad_beta_full, grad_conv, grad_gain_heads, grad_gain_second),
        ("fsdp", "seq"),
    )
    share = width // lax.axis_size("fsdp")
    offset = lax.axis_index("fsdp") * share

    def own_rows(array):
        return lax.dynamic_slice_in_dim(array, offset, share, 0)

    return (
        output,
        grad_input,
        own_rows(summed[0]),
        grad_w_qkv,
        own_rows(summed[1]),
        own_rows(summed[2]),
        summed[3],
        grad_w_out,
        own_rows(summed[4]),
        grad_w_gate_up,
        grad_down,
    )


def solution(mesh):
    in_specs = (
        P("fsdp", "seq", None),
        P("fsdp", "seq", None),
        P("fsdp"),
        P("fsdp", None),
        P("fsdp", None),
        P("fsdp", None),
        P(),
        P("fsdp", None),
        P("fsdp"),
        P("fsdp", None),
        P("fsdp", None),
    )
    out_specs = (
        P("fsdp", "seq", None),
        P("fsdp", "seq", None),
        P("fsdp"),
        P("fsdp", None),
        P("fsdp", None),
        P("fsdp", None),
        P(),
        P("fsdp", None),
        P("fsdp"),
        P("fsdp", None),
        P("fsdp", None),
    )
    return jax.shard_map(
        per_device, mesh=mesh, in_specs=in_specs, out_specs=out_specs, check_vma=False
    )
```

profile of v0, /device:TPU:0, one launch (start us, length us, event | category | flops | bytes accessed | tf_op | source)
XLA Modules:
  0.0 2502.2 jit_solution(38190960428922679)
XLA Ops:
  10.1 13.6 all-gather
  23.7 24.1 all_gather.27
  51.0 3.6 all-to-all-start.1
  54.7 25.3 %all_gather.26 = bf16[2048,12]{0,1:T(8,128)(2,1)S(1)} all-gather(bf16[256,12]{0,1:T(8,128)(2,1)S(1)} %copy-done.77), channel_id=1, replica_groups=mesh['fsdp'=8,'seq'=4] {'fsdp'}, dimensions={0}, use_global_device_ids=true | all-gather | bytes 55296 | tf_op jit(solution)/shard_map/all_gather | solution.py:130
  80.0 153.2 %all-gather.7.cloned.1.call-done = bf16[2048,6144]{1,0:T(8,128)(2,1)} async-done(((bf16[256,6144]{1,0:T(8,128)(2,1)}), bf16[2048,6144]{1,0:T(8,128)(2,1)}) %all-gather.7.cloned.1.call-update) | async-done | bytes 25165840 | tf_op jit(solution)/shard_map/all_gather | solution.py:128
  233.2 12.3 fusion.79
  251.5 5.4 fusion.82
  262.7 4.5 all-to-all-start
  268.5 12.8 all-to-all-done
  281.3 3.5 all-to-all-start.3
  287.6 11.2 all-to-all-done.3
  299.8 4.0 all-to-all-start.2
  306.9 10.2 all-to-all-done.2
  322.4 315.2 %custom-call.7 = f32[16,1,4,1,64,64]{4,5,3,2,1,0:T(8,128)S(1)} custom-call(f32[16,1,4,1,64,64]{5,4,3,2,1,0:T(8,128)} %add_bitcast_fusion), custom_call_target="InvertDiagBlocksLowerTriangular" | custom-call | tf_op jit(solution)/shard_map/jvp()/triangular_solve | solution.py:66
  637.7 4.7 multiply_bitcast_fusion.1
  645.5 3.8 fusion.83
  653.0 107.2 %while.43 = (s32[]{:T(128)}, f32[1,4,128,128]{3,2,1,0:T(8,128)S(1)}, bf16[16,1,4,64,128]{4,3,0,2,1:T(8,128)(2,1)}, f32[16,1,4,128,128]{4,3,2,1,0:T(8,128)}, f32[...) while((s32[]{:T(128)}, ...), condition=%wide.region_3.4_spmd.clone, body=%wide.region_2.3_spmd.clone.sunk | while | flops 176553984 | bytes 3148948 | solution.py:82
  760.2 3.8 copy.375
  764.0 4.3 all-to-all-start.4
  768.4 8.8 all-gather.1
  777.2 4.2 all-to-all-done.4
  796.5 6.5 multiply_reduce_fusion.8
  803.1 24.2 fusion.211
  827.3 83.8 %all-gather.13.cloned.1.call-done = bf16[5632,2048]{1,0:T(8,128)(2,1)} async-done(((bf16[704,2048]{1,0:T(8,128)(2,1)}), bf16[5632,2048]{1,0:T(8,128)(2,1)}) %all-gather.13.cloned.1.call-update) | async-done | bytes 23068688 | tf_op jit(solution)/shard_map/all_gather | solution.py:136
  911.2 18.7 multiply_convert_fusion.1
  929.9 22.1 multiply_reduce_fusion.4
  955.3 5.8 convolution_convert_fusion.4
  961.1 12.9 convolution_convert_fusion.1
  974.1 3.3 copy.381
  977.4 8.4 multiply_reduce_fusion.5
  985.8 3.8 reshape.1082
  994.0 4.0 fusion.165
  998.0 4.1 all-to-all-start.5
  1002.1 14.2 all-to-all-done.5
  1025.9 241.0 %while.44 = (s32[]{:T(128)}, f32[1,4,128,128]{2,3,1,0:T(8,128)S(1)}, f32[16,1,4,64,128]{4,3,2,1,0:T(8,128)}, f32[16,1,4,64,128]{4,3,2,1,0:T(8,128)}, f32[16,1,4,...) while((s32[]{:T(128)}, ...), condition=%wide.region_9.10_spmd.clone, body=%wide.region_8.9_spmd.clone.sunk | while | flops 352747520 | bytes 4728510 | solution.py:82
  1266.9 5.8 fusion.106
  1272.7 4.7 fusion.86
  1277.5 3.8 multiply_reduce_fusion.6
  1285.0 3.6 fusion.153
  1290.5 4.2 all-to-all-start.7
  1299.5 8.7 all-to-all-done.7
  1308.2 4.3 all-to-all-start.8
  1317.4 4.0 fusion.115
  1328.9 4.2 all-to-all-start.6
  1337.3 3.6 mul.664
  1355.8 5.9 add_add_fusion.1
  1361.8 10.6 multiply_reduce_fusion.3
  1372.4 6.3 broadcast_multiply_fusion
  1378.7 6.5 pad_add_fusion
  1387.5 3.5 slice.128
  1393.8 14.0 convolution_convert_fusion.2
  1409.4 21.2 convolution_convert_fusion
  1436.1 8.7 all_to_all.105
  1450.2 204.2 %reduce-scatter.7.cloned.1.call-done = bf16[256,6144]{1,0:T(8,128)(2,1)} async-done(((bf16[2048,6144]{1,0:T(8,128)(2,1)}), bf16[256,6144]{1,0:T(8,128)(2,1)}) %reduce-scatter.7.cloned.1.call-update) | async-done | bytes 3145744 | tf_op jit(solution)/shard_map/reduce_scatter | solution.py:98
  1654.4 444.5 %reduce-scatter.13.cloned.1.call-done = bf16[256,11264]{1,0:T(8,128)(2,1)} async-done(((bf16[2048,11264]{1,0:T(8,128)(2,1)}), bf16[256,11264]{1,0:T(8,128)(2,1)}) %reduce-scatter.13.cloned.1.call-update) | async-done | bytes 5767184
  2099.6 12.6 fusion.105
  2114.0 14.4 fusion.110
  2128.4 38.2 %all-reduce.14 = (f32[2048]{0:T(1024)S(1)}, f32[128]{0:T(128)}, f32[2048]{0:T(1024)S(1)}) all-reduce(f32[2048]{0:T(1024)S(1)} %get-tuple-element.617, f32[128]{0:T(128)S(1)} %bitcast_reduce_fusion, f32[2048]{0:T(1024)S(1)} %copy-done.78), channel_id=1, replica_groups=mesh['fsdp'=8,'seq'=4] {'fsdp','seq'}, use_global_device_ids=true, to_apply=%region_16.17 | all-reduce | flops 4224 | bytes 33792 | tf_op jit(solution)/shard_map/psum | solution.py:242
  2168.0 3.4 fusion.119
  2171.4 58.3 %all-reduce.20.cloned.1.call-done = (f32[2048,16]{0,1:T(8,128)}, f32[2048,12]{0,1:T(8,128)}) async-done(((f32[2048,16]{0,1:T(8,128)}, f32[2048,12]{0,1:T(8,128)}), (f32[2048,16]{0,1:T(8,128)}, f32[2048,12]{0,1:T(8,128)})) %all-reduce.20.cloned.1.call-update) | async-done | bytes 229392 | tf_op jit(solution)/shard_map/psum | solution.py:242
  2232.4 246.7 %all-reduce.22.cloned.1.call-done = (bf16[256,6144]{1,0:T(8,128)(2,1)}, bf16[256,2048]{1,0:T(8,128)(2,1)}, bf16[256,11264]{1,0:T(8,128)(2,1)}, bf16[704,2048]{1,0:T(8,128)(2,1)}) async-done(((bf16[256,6144]{1,0:T(8,128)(2,1)}, bf16[256,2048]{1,0:T(8,128)(2,1)}, bf16[256,11264]{1,0:T(8,128)(2,1)}, bf16[704,2048]{1,0:T(8,128)(2,1)}), (bf16[256,6144]{1,0:T(8,128)(2,1)}, bf16[256,2048]{1,0:T(8,128)(2,1)}, ...) | async-done | bytes 12845072 | tf_op jit(solution)/shard_map/psum | solution.py:104
  2479.0 5.5 convert_element_type.516
  2486.1 5.8 convert_element_type.520
  2491.9 3.3 convert_element_type.522
  (540 shorter events, 484.8 us)
Async XLA Ops:
  7.2 226.0 %all-gather.7.cloned.1.call-start = ((), (), s32[]{:S(2)}) async-start(), calls=%async_computation.14 | async-start | bytes 28311552 | tf_op jit(solution)/shard_map/all_gather | solution.py:128
  7.9 788.6 %all-gather.9.cloned.1.call-start = ((), (), s32[]{:S(2)}) async-start(), calls=%async_computation.15 | async-start | bytes 9437184 | tf_op jit(solution)/shard_map/all_gather | solution.py:131
  8.7 794.4 %all-gather.11.cloned.1.call-start = ((), (), s32[]{:S(2)}) async-start(), calls=%async_computation.16 | async-start | bytes 51904512 | tf_op jit(solution)/shard_map/all_gather | solution.py:133
  9.4 14.2 copy-start.76
  9.4 38.4 %copy-start.27 = (bf16[1,256,2048]{2,1,0:T(8,128)(2,1)S(1)}, bf16[1,256,2048]{2,1,0:T(8,128)(2,1)}, u32[]{:S(2)}) copy-start(bf16[1,256,2048]{2,1,0:T(8,128)(2,1)} %param.17) | copy-start | bytes 3145732
  9.4 901.7 %all-gather.13.cloned.1.call-start = ((), (), s32[]{:S(2)}) async-start(), calls=%async_computation.17 | async-start | bytes 25952256 | tf_op jit(solution)/shard_map/all_gather | solution.py:136
  10.1 44.6 %copy-start.77 = (bf16[256,12]{0,1:T(8,128)(2,1)S(1)}, bf16[256,12]{0,1:T(8,128)(2,1)}, u32[]{:S(2)}) copy-start(bf16[256,12]{0,1:T(8,128)(2,1)} %param.22) | copy-start | bytes 18436
  23.7 221.9 %copy-start.46 = (f32[8,1,256]{2,1,0:T(1,128)}, f32[8,1,256]{2,1,0:T(1,128)S(1)}, u32[]{:S(2)}) copy-start(f32[8,1,256]{2,1,0:T(1,128)S(1)} %convert_element_type.540) | copy-start | bytes 24580
  47.8 6.9 copy-start.48
  48.7 196.9 %copy-start.70 = (f32[256]{0:T(256)}, f32[256]{0:T(256)S(1)}, u32[]{:S(2)}) copy-start(f32[256]{0:T(256)S(1)} %fusion.204) | copy-start | bytes 3076
  51.0 211.7 %all-to-all-start.1 = ((bf16[4,2,512]{2,1,0:T(2,128)(2,1)}), bf16[4,2,512]{2,1,0:T(2,128)(2,1)S(1)}, u32[]{:S(2)}, u32[]{:S(2)}) async-start(bf16[4,2,512]{2,1,0:T(2,128)(2,1)} %reshape.1133), calls=%async_computation.1 | async-start | bytes 16384 | tf_op jit(solution)/shard_map/all_to_all | solution.py:161
  245.6 5.0 collective-permute-start
  262.7 18.6 all-to-all-start
  281.3 6.3 copy-start.38
  281.3 17.5 all-to-all-start.3
  298.8 5.8 copy-start.39
  299.8 17.3 all-to-all-start.2
  303.8 333.9 %copy-start.44 = (f32[64,64]{1,0:T(8,128)}, f32[64,64]{1,0:T(8,128)S(1)}, u32[]{:S(2)}) copy-start(f32[64,64]{1,0:T(8,128)S(1)} %fusion.200) | copy-start | bytes 49156
  637.7 7.9 copy-start.7
  760.2 8.2 copy-start.80
  760.2 8.2 copy-start.81
  764.0 17.3 all-to-all-start.4
  768.3 681.9 %reduce-scatter.9.cloned.1.call-start = ((), (), s32[]{:S(2)}) async-start(), calls=%async_computation.19 | async-start | bytes 9437184 | tf_op jit(solution)/shard_map/reduce_scatter | solution.py:98
  789.9 6.6 copy-start.19
  803.0 126.9 %copy-start.30 = (f32[256,2048]{1,0:T(8,128)}, f32[256,2048]{1,0:T(8,128)S(1)}, u32[]{:S(2)}) copy-start(f32[256,2048]{1,0:T(8,128)S(1)} %get-tuple-element.707) | copy-start | bytes 6291460
  955.2 22.1 copy-start.3
  961.1 489.1 %reduce-scatter.11.cloned.1.call-start = ((), (), s32[]{:S(2)}) async-start(), calls=%async_computation.20 | async-start | bytes 25952256 | tf_op jit(solution)/shard_map/reduce_scatter | solution.py:98
  998.0 18.3 all-to-all-start.5
  1025.9 241.0 %copy-start.8 = (f32[16,1,4,1,64,64]{4,5,3,2,1,0:T(8,128)S(1)}, f32[16,1,4,1,64,64]{4,5,3,2,1,0:T(8,128)}, u32[]{:S(2)}) copy-start(f32[16,1,4,1,64,64]{4,5,3,2,1,0:T(8,128)} %copy-done.7) | copy-start | bytes 3145732
  1266.9 5.8 copy-start.2
  1266.9 5.8 copy-start.9
  1266.9 5.8 copy-start.10
  1272.7 12.3 copy-start.6
  1290.5 17.7 all-to-all-start.7
  1297.7 14.7 copy-start.59
  1308.2 20.7 all-to-all-start.8
  1328.9 21.0 all-to-all-start.6
  1333.2 321.2 %reduce-scatter.7.cloned.1.call-start = ((), (), s32[]{:S(2)}) async-start(), calls=%async_computation.18 | async-start | bytes 28311552 | tf_op jit(solution)/shard_map/reduce_scatter | solution.py:98
  1349.9 11.9 slice-start
  1355.8 5.9 slice-start.1
  1361.8 10.7 copy-start.51
  1361.8 10.7 copy-start.53
  1361.8 10.6 copy-start.55
  1361.8 10.6 copy-start.57
  1386.2 7.6 copy-start.47
  1386.2 7.6 copy-start.71
  1386.2 6.0 collective-permute-start.1
  1393.8 14.0 copy-start.26
  1407.9 691.0 %reduce-scatter.13.cloned.1.call-start = ((), (), s32[]{:S(2)}) async-start(), calls=%async_computation.21 | async-start | bytes 51904512
  1430.7 16.8 copy-start.69
  1430.7 16.8 copy-start.28
  1430.7 799.0 %all-reduce.20.cloned.1.call-start = ((), (), s32[]{:S(2)}) async-start(), calls=%async_computation.22 | async-start | bytes 524288 | tf_op jit(solution)/shard_map/psum | solution.py:242
  1432.7 16.6 copy-start.64
  1432.7 16.6 copy-start.65
  1432.7 16.6 copy-start.66
  1432.7 16.6 copy-start.67
  1450.1 1028.9 %all-reduce.22.cloned.1.call-start = ((), (), s32[]{:S(2)}) async-start(), calls=%async_computation.23 | async-start | bytes 25690112 | tf_op jit(solution)/shard_map/psum | solution.py:104
  2099.6 12.6 copy-start.49
  2114.0 14.4 copy-start.78
  2114.0 53.9 %copy-start.75 = (f32[256]{0:T(256)S(1)}, f32[256]{0:T(256)}, u32[]{:S(2)}) copy-start(f32[256]{0:T(256)} %copy-done.74) | copy-start | bytes 3076
  2114.0 54.0 %copy-start.4 = (f32[256,2048]{1,0:T(8,128)S(1)}, f32[256,2048]{1,0:T(8,128)}, u32[]{:S(2)}) copy-start(f32[256,2048]{1,0:T(8,128)} %copy-done.3) | copy-start | bytes 6291460
  2479.0 7.1 slice-start.2
  2479.0 7.1 slice-start.3
  2486.1 5.8 copy-start.42
  (43 other events, 105.4 us)
Sparse Core Ops, SparseCore 0:
  9.7 223.4 all-gather.6
  234.8 80.2 all-gather.8
  316.8 391.8 all-gather.10
  710.1 200.9 all-gather.12
  961.2 87.8 reduce-scatter.8
  1051.2 225.7 reduce-scatter.10
  1408.0 246.3 reduce-scatter.6
  1656.8 442.0 reduce-scatter.12
  2106.1 123.5 all-reduce.19
  2234.0 244.9 all-reduce.21
where the time goes:
time: 2520 us; the launch traced here: 2500 us
  waiting for transfers between devices  1260 us (50%)
  matrix products  546 us (22%)
  other arithmetic  419 us (17%)
  blocking collectives  119 us (5%)
  local copies, waits for them, and re-layouts  103 us (4%)
  starting transfers between devices  41.7 us (2%)
    unnamed x11, waiting for transfers between devices  447 us
    another operation x5, other arithmetic, delta_rule(): lax.linalg.triangular_solve(system, targets, left_side=True, lower=True,...  318 us
    psum x1, waiting for transfers between devices, reduce_rows(): return lax.psum(summed, 'seq').astype(jnp.float32)  247 us
    reduce_scatter x3, waiting for transfers between devices, reduce_rows(): lax.psum_scatter(term(jnp.int32(0), total_rows // shards * lax.axis_size(...  204 us
    all_gather x1, waiting for transfers between devices, per_device(): lax.all_gather(w_qkv, 'fsdp', axis=0, tiled=True)  153 us
    dot_general x48, matrix products, advance(): result = jnp.einsum('shcd,shde->shce', query_part, state, precision=HIGH)  92.6 us
    dot_general x48, matrix products, advance(): jnp.einsum('shcd,shce->shde', key_raw, fresh, precision=HIGH)  90 us
    all_gather x1, waiting for transfers between devices, per_device(): down_full = lax.all_gather(w_down, 'fsdp', axis=0, tiled=True)  83.8 us
  transfers between devices with their start and end apart: 21, of which 14 were waited for; matrix products, arithmetic and copies ran while one was open for 39% of the time, Pallas kernels for 0%

commit v1 on v0

--- a/solution.py
+++ b/solution.py
@@ -8,6 +8,35 @@
 SPAN = 64
 EPS = 1e-06
 HIGH = lax.Precision.HIGHEST
+
+
+def spread_rails_up(content, d0):
+    newest = list(content.shape[1:])
+    newest[d0] *= content.shape[0]
+    arr_next = jnp.moveaxis(content, 0, d0).reshape(newest)
+    return arr_next
+
+
+def _deliver_blocks(local, row_axis):
+    world = jax.lax.axis_size(row_axis)
+    answer = local[None]
+    for to_i in range(world.bit_length() - 1):
+        response = 1 << to_i
+        queue = []
+        for jj in tuple(range(world)):
+            queue.append((jj, jj ^ response))
+        now = jax.lax.ppermute(answer, row_axis, queue)
+        carry_out = jnp.stack([answer, now])
+        main = jax.lax.axis_index(row_axis)
+        near = main >> to_i & 1
+        answer = jnp.where(near == 0, carry_out, carry_out[::-1]).reshape(-1, *local.shape)
+    return answer
+
+
+def _lay_run(local_values, local_block, array_dim):
+    z_new = _deliver_blocks(local_values, local_block)
+    w_next = spread_rails_up(z_new, array_dim)
+    return w_next
 
 
 def from_behind(array, axis, by):
@@ -133,7 +162,7 @@
         lax.all_gather(w_gate_up, "fsdp", axis=0, tiled=True),
     )
     gain_first, qkv_full, beta_full, conv_full, out_full, gain_second, gate_up_full = gathered
-    down_full = lax.all_gather(w_down, "fsdp", axis=0, tiled=True)
+    down_full = _lay_run(w_down, "fsdp", 0)
     sequences, block, width = inputs.shape
     tokens = sequences * block
     hidden_width = down_full.shape[0]

time: 2520 us -> 3550 us (1.41)
  blocking collectives: 119 us -> 1020 us
  other arithmetic: 419 us -> 494 us
  waiting for transfers between devices: 1260 us -> 1320 us
    all_gather x1, blocking collectives: 24.1 us -> 657 us  [per_device(): lax.all_gather(w_beta, 'fsdp', axis=0, tiled=True)]
    ppermute x0 -> x3, waiting for transfers between devices: none -> 327 us  [_deliver_blocks(): now = jax.lax.ppermute(answer, row_axis, queue)]
    all_gather x1, blocking collectives: 13.6 us -> 295 us  [per_device(): lax.all_gather(norm1_gain, 'fsdp', axis=0, tiled=True)]
    all_gather x1, waiting for transfers between devices: 153 us -> 0.02 us  [per_device(): lax.all_gather(w_qkv, 'fsdp', axis=0, tiled=True)]
    all_gather x1 -> x0, waiting for transfers between devices: 83.8 us -> none  [per_device(): down_full = lax.all_gather(w_down, 'fsdp', axis=0, tiled=True)]
    another operation x1 -> x5, other arithmetic: 0.01 us -> 36.6 us  [the longest x4 36.6 us: _deliver_blocks(): carry_out = jnp.stack([answer, now])]
    unnamed x11 -> x10, waiting for transfers between devices: 447 us -> 447 us
  transfers between devices with their start and end apart: 21 -> 23, of which waited for: 14 -> 12; matrix products, arithmetic and copies ran while one was open for 39% -> 29% of each run, Pallas kernels for 0% -> 0%
where the time goes in v1:
time: 3550 us; the launch traced here: 3530 us
  waiting for transfers between devices  1320 us (37%)
  blocking collectives  1020 us (29%)
  matrix products  538 us (15%)
  other arithmetic  494 us (14%)
  local copies, waits for them, and re-layouts  94.4 us (3%)
  starting transfers between devices  46.5 us (1%)
    all_gather x1, blocking collectives, per_device(): lax.all_gather(w_beta, 'fsdp', axis=0, tiled=True)  657 us
    unnamed x10, waiting for transfers between devices  447 us
    ppermute x3, waiting for transfers between devices, _deliver_blocks(): now = jax.lax.ppermute(answer, row_axis, queue)  327 us
    another operation x5, other arithmetic, delta_rule(): lax.linalg.triangular_solve(system, targets, left_side=True, lower=True,...  318 us
    all_gather x1, blocking collectives, per_device(): lax.all_gather(norm1_gain, 'fsdp', axis=0, tiled=True)  295 us
    psum x1, waiting for transfers between devices, reduce_rows(): return lax.psum(summed, 'seq').astype(jnp.float32)  247 us
    reduce_scatter x3, waiting for transfers between devices, reduce_rows(): lax.psum_scatter(term(jnp.int32(0), total_rows // shards * lax.axis_size(...  204 us
    dot_general x48, matrix products, advance(): result = jnp.einsum('shcd,shde->shce', query_part, state, precision=HIGH)  82.6 us
  transfers between devices with their start and end apart: 23, of which 12 were waited for; matrix products, arithmetic and copies ran while one was open for 29% of the time, Pallas kernels for 0%

profile of v1, /device:TPU:0, one launch (start us, length us, event | category | flops | bytes accessed | tf_op | source)
XLA Modules:
  0.0 3531.5 jit_solution(115439523687575222)
XLA Ops:
  10.9 5.0 collective-permute-done.1
  18.3 8.5 fusion.84
  30.0 321.6 %collective-permute-done.2 = bf16[2,704,2048]{2,1,0:T(8,128)(2,1)} collective-permute-done((bf16[2,704,2048]{2,1,0:T(8,128)(2,1)}, bf16[2,704,2048]{2,1,0:T(8,128)(2,1)}, u32[]{:S(2)}, u32[]{:S(2)}) %collective-permute-start.2) | collective-permute-done | bytes 5767200 | tf_op jit(solution)/shard_map/ppermute | solution.py:28
  351.6 5.9 pad_maximum_fusion.1
  357.5 6.9 reverse_select_fusion.1
  365.1 295.0 %all-gather = bf16[8,1,256]{2,1,0:T(2,128)(2,1)S(1)} all-gather(bf16[1,1,256]{2,1,0:T(2,128)(2,1)S(1)} %reshape.1120), channel_id=1, replica_groups=mesh['fsdp'=8,'seq'=4] {'fsdp'}, dimensions={0}, use_global_device_ids=true | all-gather | bytes 4608 | tf_op jit(solution)/shard_map/all_gather | solution.py:156
  660.1 656.8 %all_gather.24 = bf16[2048,16]{0,1:T(8,128)(2,1)S(1)} all-gather(bf16[256,16]{0,1:T(8,128)(2,1)S(1)} %copy-done.79), channel_id=1, replica_groups=mesh['fsdp'=8,'seq'=4] {'fsdp'}, dimensions={0}, use_global_device_ids=true | all-gather | bytes 73728 | tf_op jit(solution)/shard_map/all_gather | solution.py:158
  1320.1 3.6 all-to-all-start.1
  1323.8 13.9 all_gather.23
  1338.0 11.8 fusion.79
  1351.6 3.9 collective-permute-start
  1355.6 10.1 all-gather.1
  1368.6 5.4 fusion.82
  1377.8 3.7 all-to-all-start.2
  1382.7 4.2 fusion.166
  1388.4 7.5 all-to-all-done.2
  1395.9 4.3 all-to-all-start.3
  1407.2 6.6 all-to-all-done.3
  1413.8 3.5 all-to-all-start
  1417.3 19.9 pad_maximum_fusion
  1445.0 315.2 %custom-call.7 = f32[16,1,4,1,64,64]{4,5,3,2,1,0:T(8,128)S(1)} custom-call(f32[16,1,4,1,64,64]{5,4,3,2,1,0:T(8,128)} %add_bitcast_fusion), custom_call_target="InvertDiagBlocksLowerTriangular" | custom-call | tf_op jit(solution)/shard_map/jvp()/triangular_solve | solution.py:95
  1760.3 4.6 multiply_bitcast_fusion.1
  1768.1 3.8 fusion.85
  1776.4 97.0 %while.43 = (s32[]{:T(128)}, f32[1,4,128,128]{3,2,1,0:T(8,128)S(1)}, bf16[16,1,4,64,128]{4,3,0,2,1:T(8,128)(2,1)S(1)}, f32[16,1,4,128,128]{4,3,2,1,0:T(8,128)}, ...) while((s32[]{:T(128)}, ...), condition=%wide.region_3.4_spmd.clone, body=%wide.region_2.3_spmd.clone.sunk | while | flops 176553984 | bytes 3148948 | solution.py:111
  1875.2 4.2 all-to-all-start.4
  1879.9 28.2 reverse_select_fusion
  1919.3 7.4 multiply_reduce_fusion.8
  1926.7 24.9 fusion.212
  1951.6 28.3 multiply_convert_fusion.1
  1979.9 22.4 multiply_reduce_fusion.4
  2005.5 5.8 convolution_convert_fusion.4
  2011.4 12.5 convolution_convert_fusion.1
  2027.2 8.4 multiply_reduce_fusion.5
  2035.6 3.8 reshape.1090
  2043.2 4.0 fusion.167
  2047.2 4.5 all-to-all-start.5
  2051.7 13.0 all-to-all-done.5
  2072.9 230.3 %while.44 = (s32[]{:T(128)}, f32[1,4,128,128]{2,3,1,0:T(8,128)S(1)}, f32[16,1,4,64,128]{4,3,2,1,0:T(8,128)}, f32[16,1,4,64,128]{4,3,2,1,0:T(8,128)S(1)}, f32[16,...) while((s32[]{:T(128)}, ...), condition=%wide.region_9.10_spmd.clone, body=%wide.region_8.9_spmd.clone.sunk | while | flops 352747520 | bytes 4728510 | solution.py:111
  2303.3 3.7 fusion.158
  2308.8 4.2 all-to-all-start.8
  2313.0 3.9 fusion.131
  2317.0 6.6 fusion.88
  2323.6 3.7 multiply_reduce_fusion.6
  2329.3 4.3 fusion.108
  2338.9 4.2 all-to-all-start.7
  2348.4 8.3 all-to-all-done.7
  2356.7 3.5 all-to-all-start.6
  2386.1 5.9 add_add_fusion.1
  2392.1 10.8 multiply_reduce_fusion.3
  2403.0 6.3 broadcast_multiply_fusion
  2409.2 6.7 pad_add_fusion
  2418.2 3.5 slice.128
  2424.3 14.0 convolution_convert_fusion.2
  2439.9 21.3 convolution_convert_fusion
  2465.9 8.8 all_to_all.105
  2480.3 203.5 %reduce-scatter.7.cloned.1.call-done = bf16[256,6144]{1,0:T(8,128)(2,1)} async-done(((bf16[2048,6144]{1,0:T(8,128)(2,1)}), bf16[256,6144]{1,0:T(8,128)(2,1)}) %reduce-scatter.7.cloned.1.call-update) | async-done | bytes 3145744 | tf_op jit(solution)/shard_map/reduce_scatter | solution.py:127
  2683.9 444.5 %reduce-scatter.13.cloned.1.call-done = bf16[256,11264]{1,0:T(8,128)(2,1)} async-done(((bf16[2048,11264]{1,0:T(8,128)(2,1)}), bf16[256,11264]{1,0:T(8,128)(2,1)}) %reduce-scatter.13.cloned.1.call-update) | async-done | bytes 5767184
  3129.1 12.4 fusion.107
  3143.3 14.5 fusion.112
  3157.7 38.2 %all-reduce.14 = (f32[2048]{0:T(1024)S(1)}, f32[128]{0:T(128)}, f32[2048]{0:T(1024)S(1)}) all-reduce(f32[2048]{0:T(1024)S(1)} %get-tuple-element.617, f32[128]{0:T(128)S(1)} %bitcast_reduce_fusion, f32[2048]{0:T(1024)S(1)} %copy-done.81), channel_id=1, replica_groups=mesh['fsdp'=8,'seq'=4] {'fsdp','seq'}, use_global_device_ids=true, to_apply=%region_16.17 | all-reduce | flops 4224 | bytes 33792 | tf_op jit(solution)/shard_map/psum | solution.py:271
  3200.6 58.5 %all-reduce.20.cloned.1.call-done = (f32[2048,16]{0,1:T(8,128)}, f32[2048,12]{0,1:T(8,128)}) async-done(((f32[2048,16]{0,1:T(8,128)}, f32[2048,12]{0,1:T(8,128)}), (f32[2048,16]{0,1:T(8,128)}, f32[2048,12]{0,1:T(8,128)})) %all-reduce.20.cloned.1.call-update) | async-done | bytes 229392 | tf_op jit(solution)/shard_map/psum | solution.py:271
  3261.8 246.8 %all-reduce.22.cloned.1.call-done = (bf16[256,6144]{1,0:T(8,128)(2,1)}, bf16[256,2048]{1,0:T(8,128)(2,1)}, bf16[256,11264]{1,0:T(8,128)(2,1)}, bf16[704,2048]{1,0:T(8,128)(2,1)}) async-done(((bf16[256,6144]{1,0:T(8,128)(2,1)}, bf16[256,2048]{1,0:T(8,128)(2,1)}, bf16[256,11264]{1,0:T(8,128)(2,1)}, bf16[704,2048]{1,0:T(8,128)(2,1)}), (bf16[256,6144]{1,0:T(8,128)(2,1)}, bf16[256,2048]{1,0:T(8,128)(2,1)}, ...) | async-done | bytes 12845072 | tf_op jit(solution)/shard_map/psum | solution.py:133
  3511.6 3.8 convert_element_type.516
  3518.7 5.8 convert_element_type.520
  (559 shorter events, 478.0 us)
Async XLA Ops:
  7.2 1330.9 %all-gather.6.cloned.1.call-start = ((), (), s32[]{:S(2)}) async-start(), calls=%async_computation.14 | async-start | bytes 28311552 | tf_op jit(solution)/shard_map/all_gather | solution.py:157
  7.9 1911.3 %all-gather.8.cloned.1.call-start = ((), (), s32[]{:S(2)}) async-start(), calls=%async_computation.15 | async-start | bytes 9437184 | tf_op jit(solution)/shard_map/all_gather | solution.py:160
  8.7 1918.0 %all-gather.10.cloned.1.call-start = ((), (), s32[]{:S(2)}) async-start(), calls=%async_computation.16 | async-start | bytes 51904512 | tf_op jit(solution)/shard_map/all_gather | solution.py:162
  10.5 5.5 collective-permute-start.1
  26.8 324.8 %collective-permute-start.2 = (bf16[2,704,2048]{2,1,0:T(8,128)(2,1)}, bf16[2,704,2048]{2,1,0:T(8,128)(2,1)}, u32[]{:S(2)}, u32[]{:S(2)}) collective-permute-start(bf16[2,704,2048]{2,1,0:T(8,128)(2,1)} %get-tuple-element.694), channel_id=1, source_target_pairs={{0,8},{4,12},{8,0},{12,4},{16,24},{20,28},{24,16},{28,20},{1,9},{5... | collective-permute-start | bytes 17301512 | tf_op jit(solution)/shard_map/ppermute | solution.py:28
  357.5 302.6 %copy-start.79 = (bf16[256,16]{0,1:T(8,128)(2,1)S(1)}, bf16[256,16]{0,1:T(8,128)(2,1)}, u32[]{:S(2)}) copy-start(bf16[256,16]{0,1:T(8,128)(2,1)} %param.21) | copy-start | bytes 24580
  357.5 959.4 %copy-start.26 = (bf16[1,256,2048]{2,1,0:T(8,128)(2,1)S(1)}, bf16[1,256,2048]{2,1,0:T(8,128)(2,1)}, u32[]{:S(2)}) copy-start(bf16[1,256,2048]{2,1,0:T(8,128)(2,1)} %param.17) | copy-start | bytes 3145732
  364.5 959.3 %copy-start.80 = (bf16[256,12]{0,1:T(8,128)(2,1)S(1)}, bf16[256,12]{0,1:T(8,128)(2,1)}, u32[]{:S(2)}) copy-start(bf16[256,12]{0,1:T(8,128)(2,1)} %param.22) | copy-start | bytes 18436
  364.5 1052.8 %collective-permute-start.3 = (bf16[4,704,2048]{2,1,0:T(8,128)(2,1)}, bf16[4,704,2048]{2,1,0:T(8,128)(2,1)}, u32[]{:S(2)}, u32[]{:S(2)}) collective-permute-start(bf16[4,704,2048]{2,1,0:T(8,128)(2,1)} %bitcast.56), channel_id=1, source_target_pairs={{0,16},{4,20},{8,24},{12,28},{16,0},{20,4},{24,8},{28,12},{1,17},{... | collective-permute-start | bytes 34603016 | tf_op jit(solution)/shard_map/ppermute | solution.py:28
  660.1 689.7 %copy-start.49 = (f32[8,1,256]{2,1,0:T(1,128)}, f32[8,1,256]{2,1,0:T(1,128)S(1)}, u32[]{:S(2)}) copy-start(f32[8,1,256]{2,1,0:T(1,128)S(1)} %convert_element_type.540) | copy-start | bytes 24580
  1317.8 32.1 copy-start.73
  1320.1 57.6 %all-to-all-start.1 = ((bf16[4,2,512]{2,1,0:T(2,128)(2,1)}), bf16[4,2,512]{2,1,0:T(2,128)(2,1)S(1)}, u32[]{:S(2)}, u32[]{:S(2)}) async-start(bf16[4,2,512]{2,1,0:T(2,128)(2,1)} %reshape.1141), calls=%async_computation.1 | async-start | bytes 16384 | tf_op jit(solution)/shard_map/all_to_all | solution.py:190
  1337.9 104.1 %copy-start.47 = (f32[64,64]{1,0:T(8,128)}, f32[64,64]{1,0:T(8,128)S(1)}, u32[]{:S(2)}) copy-start(f32[64,64]{1,0:T(8,128)S(1)} %broadcast_select_fusion) | copy-start | bytes 49156
  1338.0 30.6 copy-start.53
  1338.0 30.6 copy-start.55
  1338.0 30.6 copy-start.57
  1338.0 30.6 copy-start.59
  1338.0 17.6 copy-start.85
  1338.0 17.6 copy-start.86
  1351.6 14.2 collective-permute-start
  1355.5 404.8 %copy-start.45 = (f32[64,64]{1,0:T(8,128)}, f32[64,64]{1,0:T(8,128)S(1)}, u32[]{:S(2)}) copy-start(f32[64,64]{1,0:T(8,128)S(1)} %fusion.201) | copy-start | bytes 49156
  1355.6 25.9 copy-start.82
  1377.8 18.1 all-to-all-start.2
  1382.7 59.3 %copy-start.70 = (pred[64,64]{1,0:T(8,128)(4,1)}, pred[64,64]{1,0:T(8,128)(4,1)S(1)}, u32[]{:S(2)}) copy-start(pred[64,64]{1,0:T(8,128)(4,1)S(1)} %get-tuple-element.716) | copy-start | bytes 12292
  1386.9 18.2 copy-start.17
  1395.9 17.9 all-to-all-start.3
  1400.9 366.5 %copy-start.42 = (f32[16,4,64]{2,1,0:T(4,128)}, f32[16,4,64]{2,1,0:T(4,128)S(1)}, u32[]{:S(2)}) copy-start(f32[16,4,64]{2,1,0:T(4,128)S(1)} %copy.364) | copy-start | bytes 49156
  1405.1 8.7 copy-start.63
  1413.8 27.4 all-to-all-start
  1441.3 326.1 %copy-start.1 = (bf16[1,4,256,4,128]{4,2,1,3,0:T(8,128)(2,1)}, bf16[1,4,256,4,128]{4,2,1,3,0:T(8,128)(2,1)S(1)}, u32[]{:S(2)}) copy-start(bf16[1,4,256,4,128]{4,2,1,3,0:T(8,128)(2,1)S(1)} %copy.360) | copy-start | bytes 3145732
  1760.3 7.9 copy-start.9
  1875.2 32.9 all-to-all-start.4
  1879.5 600.9 %reduce-scatter.9.cloned.1.call-start = ((), (), s32[]{:S(2)}) async-start(), calls=%async_computation.18 | async-start | bytes 9437184 | tf_op jit(solution)/shard_map/reduce_scatter | solution.py:127
  1926.7 24.9 copy-start.37
  1951.6 28.4 copy-start.29
  2005.5 21.7 copy-start.5
  2011.3 469.0 %reduce-scatter.11.cloned.1.call-start = ((), (), s32[]{:S(2)}) async-start(), calls=%async_computation.19 | async-start | bytes 25952256 | tf_op jit(solution)/shard_map/reduce_scatter | solution.py:127
  2047.2 17.5 all-to-all-start.5
  2072.9 230.3 %copy-start.2 = (bf16[1,4,256,4,128]{4,2,1,3,0:T(8,128)(2,1)S(1)}, bf16[1,4,256,4,128]{4,2,1,3,0:T(8,128)(2,1)}, u32[]{:S(2)}) copy-start(bf16[1,4,256,4,128]{4,2,1,3,0:T(8,128)(2,1)} %copy-done.1) | copy-start | bytes 3145732
  2072.9 230.3 %copy-start.46 = (f32[64,64]{1,0:T(8,128)S(1)}, f32[64,64]{1,0:T(8,128)}, u32[]{:S(2)}) copy-start(f32[64,64]{1,0:T(8,128)} %copy-done.45) | copy-start | bytes 49156
  2308.8 30.1 all-to-all-start.8
  2338.9 17.8 all-to-all-start.7
  2346.6 13.6 copy-start.62
  2356.7 16.6 all-to-all-start.6
  2360.2 323.7 %reduce-scatter.7.cloned.1.call-start = ((), (), s32[]{:S(2)}) async-start(), calls=%async_computation.17 | async-start | bytes 28311552 | tf_op jit(solution)/shard_map/reduce_scatter | solution.py:127
  2381.5 10.6 slice-start
  2392.1 10.9 copy-start.54
  2392.1 10.9 copy-start.56
  2392.1 10.9 copy-start.58
  2392.1 10.9 copy-start.60
  2416.9 6.0 collective-permute-start.4
  2424.3 14.0 copy-start.25
  2438.3 690.1 %reduce-scatter.13.cloned.1.call-start = ((), (), s32[]{:S(2)}) async-start(), calls=%async_computation.20 | async-start | bytes 51904512
  2461.2 16.9 copy-start.28
  2461.2 798.0 %all-reduce.20.cloned.1.call-start = ((), (), s32[]{:S(2)}) async-start(), calls=%async_computation.21 | async-start | bytes 524288 | tf_op jit(solution)/shard_map/psum | solution.py:271
  2462.5 16.7 copy-start.67
  2462.5 16.7 copy-start.68
  2462.5 16.7 copy-start.69
  2480.0 1028.6 %all-reduce.22.cloned.1.call-start = ((), (), s32[]{:S(2)}) async-start(), calls=%async_computation.22 | async-start | bytes 25690112 | tf_op jit(solution)/shard_map/psum | solution.py:133
  3129.1 12.4 copy-start.52
  3143.2 14.5 copy-start.81
  3143.2 53.9 %copy-start.78 = (f32[256]{0:T(256)S(1)}, f32[256]{0:T(256)}, u32[]{:S(2)}) copy-start(f32[256]{0:T(256)} %copy-done.77) | copy-start | bytes 3076
  3143.3 53.9 %copy-start.6 = (f32[256,2048]{1,0:T(8,128)S(1)}, f32[256,2048]{1,0:T(8,128)}, u32[]{:S(2)}) copy-start(f32[256,2048]{1,0:T(8,128)} %copy-done.5) | copy-start | bytes 6291460
  3508.6 10.1 slice-start.2
  (50 other events, 180.7 us)
Sparse Core Ops, SparseCore 0:
  9.7 339.8 all-gather.5
  351.2 366.5 all-gather.7
  719.4 577.0 all-gather.9
  2011.4 88.2 reduce-scatter.8
  2101.9 225.7 reduce-scatter.10
  2438.4 245.3 reduce-scatter.6
  2686.3 442.0 reduce-scatter.12
  3135.6 123.5 all-reduce.19
  3263.6 244.9 all-reduce.21
